TPU v7x, 256 devices: a whole 4x4x8 slice. The times are simulated.
256 devices in a mesh: tgt: 4 (over z_lo, core), sup: 64 (over y, x, z_hi).
Axes of the slice: x: 4, y: 4, z: 8 (z_hi: 4, z_lo: 2; z = z_hi * 2 + z_lo), core: 2. Of those that a mesh axis runs over, the one named last changes fastest.
Arguments:
- support_images: bfloat16 [512, 3072], P('sup'), may hold values from -6 to 6
- target_images: bfloat16 [262144, 3072], P(('tgt', 'sup')), may hold values from -6 to 6
- support_labels: int32 [512], replicated, may hold values from 0 to 99
- target_labels: int32 [262144], P(('tgt', 'sup')), may hold values from 0 to 99
Outputs:
- scaled_grad: float32 [512, 3072], P('sup')
- loss: float32 [], replicated
All inputs are finite; a program needn't handle non-finite values.
Results may differ from a plain program's by a relative error of at most 0.0095.
Values may be sent and summed in bfloat16 or wider, within the bound.
A program may use at most 128 MiB of HBM per device.

v0:
```python
import math
import jax
import jax.numpy as jnp
from jax import lax
from jax.sharding import PartitionSpec as P

D = 3072
C = 100
LAYERS = 5
ridge_scale = 0.1
two_over_pi = 2.0 / math.pi


def ntk_kernel(gram_in, norm_row, norm_col):
    tangent = gram_in
    for layer_no in range(LAYERS):
        spread = (1.0 + 2.0 * norm_row) * (1.0 + 2.0 * norm_col)
        new_gram = two_over_pi * jnp.arcsin(2.0 * gram_in / jnp.sqrt(spread))
        slope_term = 2.0 * two_over_pi / jnp.sqrt(spread - 4.0 * gram_in * gram_in)
        tangent = new_gram + tangent * slope_term
        norm_row = two_over_pi * jnp.arcsin(2.0 * norm_row / (1.0 + 2.0 * norm_row))
        norm_col = two_over_pi * jnp.arcsin(2.0 * norm_col / (1.0 + 2.0 * norm_col))
        gram_in = new_gram
    return tangent


def ridge_solve(factor, rhs_block):
    middle = lax.linalg.triangular_solve(factor, rhs_block, left_side=True, lower=True)
    return lax.linalg.triangular_solve(factor, middle, left_side=True, lower=True, transpose_a=True)


def make_terms(
    coef_ts, coef_ss, target_images, support_images, rows_sup, column_scale, first_group
):
    back_dims = (((0,), (0,)), ((), ()))

    def term_rows(start, row_count):
        result = lax.dot_general(
            coef_ts, target_images, back_dims, preferred_element_type=jnp.float32
        )
        result = result + first_group * lax.dot_general(
            coef_ss, support_images, back_dims, preferred_element_type=jnp.float32
        )
        return result + column_scale[:, None] * rows_sup.astype(jnp.float32)

    return term_rows


def body(support_images, target_images, support_labels, target_labels):
    sup_rows = support_images.shape[0]
    tgt_rows = target_images.shape[0]
    n_sup = lax.axis_size("sup")
    n_tgt = lax.axis_size("tgt")
    total_sup = sup_rows * n_sup
    total_tgt = tgt_rows * n_sup * n_tgt
    contract = (((1,), (1,)), ((), ()))
    gathered = lax.all_gather(support_images, "sup", axis=0, tiled=True)
    norm_all = jnp.sum(jnp.square(gathered.astype(jnp.float32)), axis=1) / D
    norm_own = jnp.sum(jnp.square(support_images.astype(jnp.float32)), axis=1) / D
    norm_tgt = jnp.sum(jnp.square(target_images.astype(jnp.float32)), axis=1) / D
    gram_ts = (
        lax.dot_general(target_images, gathered, contract, preferred_element_type=jnp.float32) / D
    )
    gram_ss = (
        lax.dot_general(support_images, gathered, contract, preferred_element_type=jnp.float32) / D
    )
    kern_ts, pull_ts = jax.vjp(ntk_kernel, gram_ts, norm_tgt[:, None], norm_all[None, :])
    kern_own, pull_ss = jax.vjp(ntk_kernel, gram_ss, norm_own[:, None], norm_all[None, :])
    kern_ss = lax.all_gather(kern_own, "sup", axis=0, tiled=True)
    trace_mean = jnp.trace(kern_ss) / total_sup
    system = kern_ss + ridge_scale * trace_mean * jnp.eye(total_sup, dtype=jnp.float32)
    factor = jnp.linalg.cholesky(system)
    classes = jnp.arange(C, dtype=jnp.int32)
    label_sup = (support_labels[:, None] == classes[None, :]).astype(jnp.float32) - 1.0 / C
    label_tgt = (target_labels[:, None] == classes[None, :]).astype(jnp.float32) - 1.0 / C
    coeffs = ridge_solve(factor, label_sup)
    misfit = jnp.dot(kern_ts, coeffs, precision=lax.Precision.HIGHEST) - label_tgt
    loss_part = jnp.sum(misfit * misfit) / (2.0 * total_tgt)
    d_predict = misfit / total_tgt
    d_coeff_part = jnp.dot(kern_ts.T, d_predict, precision=lax.Precision.HIGHEST)
    d_coeffs, loss_value = lax.psum((d_coeff_part, loss_part), ("tgt", "sup"))
    adjoint = ridge_solve(factor, d_coeffs)
    ridge_grad = -ridge_scale / total_sup * jnp.sum(adjoint * coeffs)
    start_own = lax.axis_index("sup") * sup_rows
    adjoint_own = lax.dynamic_slice_in_dim(adjoint, start_own, sup_rows, 0)
    row_ids = start_own + jnp.arange(sup_rows, dtype=jnp.int32)
    col_ids = jnp.arange(total_sup, dtype=jnp.int32)
    diagonal = (row_ids[:, None] == col_ids[None, :]).astype(jnp.float32)
    d_kern_own = (
        -jnp.dot(adjoint_own, coeffs.T, precision=lax.Precision.HIGHEST) + ridge_grad * diagonal
    )
    d_kern_ts = jnp.dot(d_predict, coeffs.T, precision=lax.Precision.HIGHEST)
    g_ts, unused_tgt, qcol_ts = pull_ts(d_kern_ts)
    g_ss, qrow_ss, qcol_ss = pull_ss(d_kern_own)
    first_group = (lax.axis_index("tgt") == 0).astype(jnp.float32)
    coef_ts = (g_ts / D).astype(jnp.bfloat16)
    coef_ss = (g_ss / D).astype(jnp.bfloat16)
    column_scale = 2.0 / D * (qcol_ts[0] + first_group * qcol_ss[0])
    term_rows = make_terms(
        coef_ts, coef_ss, target_images, support_images, gathered, column_scale, first_group
    )
    partial_rows = lax.psum_scatter(
        term_rows(jnp.int32(0), sup_rows * lax.axis_size("sup")),
        "sup",
        scatter_dimension=0,
        tiled=True,
    )
    summed = lax.psum(partial_rows, "tgt")
    local_rows = jnp.dot(coef_ss, gathered, preferred_element_type=jnp.float32)
    local_rows = local_rows + 2.0 / D * qrow_ss * support_images.astype(jnp.float32)
    return (total_sup * (summed + local_rows), loss_value)


def solution(mesh):
    in_specs = (P("sup", None), P(("tgt", "sup"), None), P(), P(("tgt", "sup")))
    out_specs = (P("sup", None), P())
    return jax.shard_map(body, mesh=mesh, in_specs=in_specs, out_specs=out_specs, check_vma=False)
```

profile of v0, /device:TPU:1, one launch (start us, length us, event | category | flops | bytes accessed | tf_op | source)
XLA Modules:
  0.0 937.1 jit_solution(4720406489037573649)
XLA Ops:
  10.6 4.1 multiply_reduce_fusion
  15.8 82.0 %all-gather.3.cloned.1.call-done = bf16[512,3072]{1,0:T(8,128)(2,1)} async-done(((bf16[8,3072]{1,0:T(8,128)(2,1)}), bf16[512,3072]{1,0:T(8,128)(2,1)}) %all-gather.3.cloned.1.call-update) | async-done | bytes 3145744 | tf_op jit(solution)/shard_map/all_gather | solution.py:57
  97.8 2.7 fusion
  101.4 1.8 multiply_add_fusion.5
  103.5 36.9 %multiply_add_fusion = (f32[1024,512]{1,0:T(8,128)}, f32[1024,512]{1,0:T(8,128)}, f32[1024,512]{1,0:T(8,128)}, f32[1024,512]{1,0:T(8,128)}) fusion(f32[512]{0:T(512)S(1)} %get-tuple-element.154, f32[1024]{0:T(1024)S(1)} %multiply_add_fusion.10, f32[512]{0:T(512)S(1)} %get-tuple-element.119, f32[1024]{0:T(1024)S(1)} %get-tuple-element.135, ...), kind=kOutput, calls=%fused_computation.109 | convolution fusion | flops 3261071360 | bytes 17856512 | tf_op jit(solution)/shard_map/dot_general | solution.py:62
  140.5 35.2 %all-gather.5.cloned.1.call-done = f32[512,512]{1,0:T(8,128)} async-done(((f32[8,512]{1,0:T(8,128)}), f32[512,512]{1,0:T(8,128)}) %all-gather.5.cloned.1.call-update) | async-done | bytes 1048592 | tf_op jit(solution)/shard_map/all_gather | solution.py:69
  175.7 2.5 copy.23
  178.2 1.9 select_reduce_fusion
  180.8 2.3 select_add_fusion
  183.1 2.6 copy.24
  185.7 1.8 fusion.99
  187.5 1.0 copy-done.3
  188.5 11.7 %cholesky.103 = f32[128,128]{1,0:T(8,128)S(1)} custom-call(f32[128,128]{1,0:T(8,128)S(1)} %cholesky.263), custom_call_target="Cholesky" | custom-call | tf_op jit(solution)/shard_map/jit(cholesky)/cholesky | solution.py:72
  200.9 9.8 %custom-call.33 = f32[1,128,128]{1,2,0:T(8,128)S(1)} custom-call(f32[1,128,128]{2,1,0:T(8,128)S(1)} %get-tuple-element.131), custom_call_target="InvertDiagBlocksLowerTriangular" | custom-call | tf_op jit(solution)/shard_map/jit(cholesky)/cholesky | solution.py:72
  210.7 1.2 fusion.110
  211.9 1.3 convolution_subtract_fusion.1
  213.9 11.7 %cholesky.215 = f32[128,128]{1,0:T(8,128)S(1)} custom-call(f32[128,128]{1,0:T(8,128)S(1)} %cholesky.267), custom_call_target="Cholesky" | custom-call | tf_op jit(solution)/shard_map/jit(cholesky)/cholesky | solution.py:72
  225.6 1.2 select_reduce_fusion.3
  228.6 1.1 cholesky.222
  229.6 11.0 %custom-call.34 = f32[1,128,128]{1,2,0:T(8,128)S(1)} custom-call(f32[1,128,128]{2,1,0:T(8,128)} %get-tuple-element.129), custom_call_target="InvertDiagBlocksLowerTriangular" | custom-call | tf_op jit(solution)/shard_map/jit(cholesky)/cholesky | solution.py:72
  241.4 1.5 constant_dynamic-update-slice_fusion.2
  242.8 1.9 convolution_dynamic-update-slice_fusion
  244.7 1.6 convolution_subtract_fusion.2
  246.4 11.7 %cholesky.236 = f32[128,128]{1,0:T(8,128)S(1)} custom-call(f32[128,128]{1,0:T(8,128)S(1)} %cholesky.272), custom_call_target="Cholesky" | custom-call | tf_op jit(solution)/shard_map/jit(cholesky)/cholesky | solution.py:72
  258.9 9.8 %custom-call.35 = f32[1,128,128]{1,2,0:T(8,128)S(1)} custom-call(f32[1,128,128]{2,1,0:T(8,128)S(1)} %get-tuple-element.127), custom_call_target="InvertDiagBlocksLowerTriangular" | custom-call | tf_op jit(solution)/shard_map/jit(cholesky)/cholesky | solution.py:72
  269.6 1.5 convolution_subtract_fusion.6
  271.1 11.9 %cholesky.253 = f32[128,128]{1,0:T(8,128)S(1)} custom-call(f32[128,128]{1,0:T(8,128)S(1)} %convolution_subtract_fusion.6), custom_call_target="Cholesky" | custom-call | tf_op jit(solution)/shard_map/jit(cholesky)/cholesky | solution.py:72
  288.9 2.4 select_select_fusion
  291.3 14.5 %while.8 = (s32[]{:T(128)}, f32[512,512]{0,1:T(8,128)}, s32[4,2]{0,1:T(2,128)S(1)}, f32[4,128,128]{2,1,0:T(8,128)}, s32[]{:T(128)}) while((s32[]{:T(128)}, f32[512,512]{0,1:T(8,128)}, s32[4,2]{0,1:T(2,128)S(1)}, f32[4,128,128]{2,1,0:T(8,128)}, s32[]{:T(128)}) %tuple.98), condition=%wide.while_cond.1, body=%wide.while_body.1.sunk | while | flops 2 | bytes 393829 | solution.py:29
  291.9 2.3 dynamic-slice.14
  295.6 2.3 dynamic-slice.14
  299.2 2.3 dynamic-slice.14
  302.8 2.2 dynamic-slice.14
  305.7 40.1 %custom-call.39 = f32[4,128,128]{1,2,0:T(8,128)S(1)} custom-call(f32[4,128,128]{2,1,0:T(8,128)} %get-tuple-element.33), custom_call_target="InvertDiagBlocksLowerTriangular" | custom-call | tf_op jit(solution)/shard_map/triangular_solve/custom-call.8 | solution.py:29
  345.9 1.3 fusion.155
  347.2 1.2 convolution_subtract_fusion.4
  348.6 1.3 convolution_subtract_fusion.3
  350.2 1.4 convolution_subtract_fusion.5
  352.2 1.1 convolution_subtract_fusion.12
  353.6 1.2 convolution_subtract_fusion.11
  355.0 1.3 convolution_subtract_fusion.15
  356.7 2.8 multiply_reduce_fusion.1
  360.2 2.1 fusion.102
  362.5 18.7 %fusion.81 = (f32[1024,512]{1,0:T(8,128)S(1)}, f32[1024,512]{1,0:T(8,128)S(1)}, f32[1024,512]{1,0:T(8,128)S(1)}) fusion(f32[512]{0:T(512)} %copy-done.32, f32[1024]{0:T(1024)} %copy-done.50, f32[512]{0:T(512)S(1)} %copy-done.20, f32[1024]{0:T(1024)} %copy-done.38, f32[1024,512]{1,0:T(8,128)} %get-tuple-element.115, f32[512]{0:T(512)S(1)} %copy-done.22, ...), kind=kOutput, calls=%fused_computation.97 | convolution fusion | flops 658761728 | bytes 11118592 | tf_op jit(solution)/shard_map/dot_general | solution.py:92
  381.3 26.9 %fusion.92 = (f32[512]{0:T(512)}, f32[512]{0:T(512)}, f32[512]{0:T(512)}, f32[1024,512]{1,0:T(8,128)S(1)}, f32[1024,512]{1,0:T(8,128)S(1)}) fusion(f32[512]{0:T(512)S(1)} %copy-done.33, f32[1024]{0:T(1024)S(1)} %copy-done.51, f32[1024,512]{1,0:T(8,128)S(1)} %get-tuple-element.151, f32[1024,512]{1,0:T(8,128)S(1)} %copy-done.58, f32[512]{0:T(512)S(1)} %copy-done.20, ...), kind=kLoop, calls=%fused_computation.128 | loop fusion | flops 67107328 | bytes 16814080 | tf_op jit(solution)/shard_map/transpose(jvp())/reduce_sum | solution.py:17
  408.2 14.4 %fusion.61 = (f32[1024,512]{1,0:T(8,128)S(1)}, f32[1024,512]{1,0:T(8,128)S(1)}) fusion(f32[1024,512]{1,0:T(8,128)S(1)} %get-tuple-element.92, f32[1024,512]{1,0:T(8,128)S(1)} %get-tuple-element.91, f32[1024,512]{1,0:T(8,128)S(1)} %copy-done.4, f32[512]{0:T(512)S(1)} %copy-done.22, f32[1024]{0:T(1024)S(1)} %copy-done.37, f32[512]{0:T(512)S(1)} %copy-done.17, ...), kind=kLoop, calls=%fused_computation.77 | loop fusion | flops 24117248 | bytes 14704640 | tf_op jit(solution)/shard_map/transpose(jvp())/mul | solution.py:18
  422.6 12.5 %fusion.89 = (f32[512]{0:T(512)}, f32[512]{0:T(512)}, f32[1024,512]{1,0:T(8,128)S(1)}) fusion(f32[1024,512]{1,0:T(8,128)S(1)} %get-tuple-element.103, f32[512]{0:T(512)S(1)} %copy-done.17, f32[1024]{0:T(1024)S(1)} %copy-done.26, f32[1024,512]{1,0:T(8,128)S(1)} %get-tuple-element.104, f32[1024,512]{1,0:T(8,128)S(1)} %copy-done.2, f32[512]{0:T(512)S(1)} %copy-done.15, ...), kind=kLoop, calls=%fused_computation.125 | loop fusion | flops 36699136 | bytes 8404992 | tf_op jit(solution)/shard_map/transpose(jvp())/reduce_sum | solution.py:17
  435.1 14.1 %fusion.100 = f32[512,3072]{1,0:T(8,128)} fusion(bf16[1024,3072]{1,0:T(8,128)(2,1)S(1)} %bitcast.103, f32[1024,512]{1,0:T(8,128)S(1)} %get-tuple-element.93, f32[1024,512]{1,0:T(8,128)S(1)} %copy-done.2, f32[512]{0:T(512)S(1)} %copy-done.15, f32[1024]{0:T(1024)S(1)} %copy-done.24, f32[1024,512]{1,0:T(8,128)S(1)} %get-tuple-element.104, ...), kind=kOutput, calls=%fused_computation.161 | convolution fusion | flops 3242196992 | bytes 18886656 | tf_op jit(solution)/shard_map/dot_general | solution.py:38
  449.1 157.9 %all-reduce.4.cloned.1.call-done = f32[512,100]{0,1:T(8,128)} async-done(((f32[512,100]{0,1:T(8,128)}), f32[512,100]{0,1:T(8,128)}) %all-reduce.4.cloned.1.call-update) | async-done | bytes 204816 | tf_op jit(solution)/shard_map/psum | solution.py:81
  607.0 1.1 fusion.166
  608.1 1.1 convolution_subtract_fusion.10
  609.4 1.2 convolution_subtract_fusion.9
  611.0 1.3 convolution_subtract_fusion.14
  612.8 1.1 convolution_subtract_fusion.8
  614.2 1.2 convolution_subtract_fusion.7
  615.6 1.3 convolution_subtract_fusion.13
  618.6 1.3 fusion.209
  619.9 1.1 multiply_reduce_fusion.6
  621.0 1.1 multiply_reduce_fusion.5
  625.4 6.9 fusion.1
  633.1 78.1 %psum.23 = f32[]{:T(128)} all-reduce(f32[]{:T(128)S(6)} %div.757), channel_id=1, replica_groups=mesh['tgt'=4,'sup'=64] {'tgt','sup'}, use_global_device_ids=true, to_apply=%region_32.35 | all-reduce | flops 1 | bytes 8 | tf_op jit(solution)/shard_map/psum | solution.py:81
  711.2 174.7 %reduce-scatter.2.cloned.1.call-done = f32[8,3072]{1,0:T(8,128)} async-done(((f32[512,3072]{1,0:T(8,128)}), f32[8,3072]{1,0:T(8,128)}) %reduce-scatter.2.cloned.1.call-update) | async-done | bytes 98320 | tf_op jit(solution)/shard_map/reduce_scatter | solution.py:102
  886.0 42.1 %all-reduce.6.cloned.1.call-done = f32[8,3072]{1,0:T(8,128)} async-done(((f32[8,3072]{1,0:T(8,128)}), f32[8,3072]{1,0:T(8,128)}) %all-reduce.6.cloned.1.call-update) | async-done | bytes 98320 | tf_op jit(solution)/shard_map/psum | solution.py:108
  928.1 2.2 fusion.3
  (200 shorter events, 28.6 us)
Async XLA Ops:
  7.2 90.6 %all-gather.3.cloned.1.call-start = ((), (), s32[]{:S(2)}) async-start(), calls=%async_computation.1 | async-start | bytes 3194880 | tf_op jit(solution)/shard_map/all_gather | solution.py:57
  7.9 167.8 %all-gather.5.cloned.1.call-start = ((), (), s32[]{:S(2)}) async-start(), calls=%async_computation.2 | async-start | bytes 1064960 | tf_op jit(solution)/shard_map/all_gather | solution.py:69
  9.9 0.5 copy-start.42
  10.1 4.6 copy-start.53
  10.1 91.2 %copy-start.27 = (f32[8]{0:T(128)}, f32[8]{0:T(128)S(1)}, u32[]{:S(2)}) copy-start(f32[8]{0:T(128)S(1)} %get-tuple-element.148) | copy-start | bytes 100
  10.1 91.2 %copy-start.40 = (f32[8]{0:T(128)}, f32[8]{0:T(128)S(1)}, u32[]{:S(2)}) copy-start(f32[8]{0:T(128)S(1)} %get-tuple-element.110) | copy-start | bytes 100
  10.1 91.2 %copy-start.34 = (f32[8]{0:T(128)}, f32[8]{0:T(128)S(1)}, u32[]{:S(2)}) copy-start(f32[8]{0:T(128)S(1)} %broadcast_add_fusion.8) | copy-start | bytes 100
  10.6 90.7 %copy-start.41 = (f32[8]{0:T(128)}, f32[8]{0:T(128)S(1)}, u32[]{:S(2)}) copy-start(f32[8]{0:T(128)S(1)} %get-tuple-element.156) | copy-start | bytes 100
  10.6 90.7 %copy-start.48 = (f32[8]{0:T(128)}, f32[8]{0:T(128)S(1)}, u32[]{:S(2)}) copy-start(f32[8]{0:T(128)S(1)} %get-tuple-element.155) | copy-start | bytes 100
  10.6 4.4 copy-start.52
  14.7 86.6 %copy-start.6 = (bf16[8,3072]{1,0:T(8,128)(2,1)S(1)}, bf16[8,3072]{1,0:T(8,128)(2,1)}, u32[]{:S(2)}) copy-start(bf16[8,3072]{1,0:T(8,128)(2,1)} %param.8) | copy-start | bytes 147460
  14.9 88.5 %copy-start.23 = (f32[1024]{0:T(1024)}, f32[1024]{0:T(1024)S(1)}, u32[]{:S(2)}) copy-start(f32[1024]{0:T(1024)S(1)} %get-tuple-element.133) | copy-start | bytes 12292
  14.9 88.5 %copy-start.25 = (f32[1024]{0:T(1024)}, f32[1024]{0:T(1024)S(1)}, u32[]{:S(2)}) copy-start(f32[1024]{0:T(1024)S(1)} %get-tuple-element.137) | copy-start | bytes 12292
  14.9 88.5 %copy-start.36 = (f32[1024]{0:T(1024)}, f32[1024]{0:T(1024)S(1)}, u32[]{:S(2)}) copy-start(f32[1024]{0:T(1024)S(1)} %get-tuple-element.134) | copy-start | bytes 12292
  14.9 88.5 %copy-start.38 = (f32[1024]{0:T(1024)}, f32[1024]{0:T(1024)S(1)}, u32[]{:S(2)}) copy-start(f32[1024]{0:T(1024)S(1)} %get-tuple-element.135) | copy-start | bytes 12292
  15.0 88.5 %copy-start.50 = (f32[1024]{0:T(1024)}, f32[1024]{0:T(1024)S(1)}, u32[]{:S(2)}) copy-start(f32[1024]{0:T(1024)S(1)} %multiply_add_fusion.10) | copy-start | bytes 12292
  97.8 3.6 copy-start
  100.5 0.6 copy-start.31
  100.7 0.6 copy-start.29
  100.7 0.6 copy-start.30
  100.7 39.7 %copy-start.14 = (f32[512]{0:T(512)}, f32[512]{0:T(512)S(1)}, u32[]{:S(2)}) copy-start(f32[512]{0:T(512)S(1)} %get-tuple-element.145) | copy-start | bytes 6148
  100.7 39.7 %copy-start.19 = (f32[512]{0:T(512)}, f32[512]{0:T(512)S(1)}, u32[]{:S(2)}) copy-start(f32[512]{0:T(512)S(1)} %get-tuple-element.119) | copy-start | bytes 6148
  101.2 39.3 %copy-start.16 = (f32[512]{0:T(512)}, f32[512]{0:T(512)S(1)}, u32[]{:S(2)}) copy-start(f32[512]{0:T(512)S(1)} %get-tuple-element.146) | copy-start | bytes 6148
  101.2 39.3 %copy-start.21 = (f32[512]{0:T(512)}, f32[512]{0:T(512)S(1)}, u32[]{:S(2)}) copy-start(f32[512]{0:T(512)S(1)} %get-tuple-element.147) | copy-start | bytes 6148
  101.2 39.3 %copy-start.32 = (f32[512]{0:T(512)}, f32[512]{0:T(512)S(1)}, u32[]{:S(2)}) copy-start(f32[512]{0:T(512)S(1)} %get-tuple-element.154) | copy-start | bytes 6148
  103.2 503.8 %all-reduce.4.cloned.1.call-start = ((), (), s32[]{:S(2)}) async-start(), calls=%async_computation.3 | async-start | bytes 425984 | tf_op jit(solution)/shard_map/psum | solution.py:81
  187.5 1.1 copy-start.3
  200.2 0.6 copy-start.13
  213.2 0.7 copy-start.10
  241.3 41.8 %copy-start.56 = (f32[128]{0:T(128)S(1)}, f32[128]{0:T(128)}, u32[]{:S(2)}) copy-start(f32[128]{0:T(128)} %get-tuple-element.128) | copy-start | bytes 1540
  241.3 42.5 %copy-start.55 = (f32[128]{0:T(128)S(1)}, f32[128]{0:T(128)}, u32[]{:S(2)}) copy-start(f32[128]{0:T(128)} %get-tuple-element.130) | copy-start | bytes 1540
  244.7 46.6 %copy-start.57 = (s32[4]{0:T(128)S(1)}, s32[4]{0:T(128)}, u32[]{:S(2)}) copy-start(s32[4]{0:T(128)} %iota_multiply_fusion) | copy-start | bytes 52
  305.7 50.9 %copy-start.49 = (s32[1024]{0:T(1024)S(1)}, s32[1024]{0:T(1024)}, u32[]{:S(2)}) copy-start(s32[1024]{0:T(1024)} %param.11) | copy-start | bytes 12292
  345.9 10.8 %copy-start.1 = (f32[1024,512]{1,0:T(8,128)S(1)}, f32[1024,512]{1,0:T(8,128)}, u32[]{:S(2)}) copy-start(f32[1024,512]{1,0:T(8,128)} %get-tuple-element.114) | copy-start | bytes 6291460
  355.0 1.6 copy-start.8
  356.6 2.9 copy-start.11
  359.5 0.8 copy-start.5
  359.5 2.9 copy-start.20
  359.5 2.9 copy-start.22
  362.3 523.6 %reduce-scatter.2.cloned.1.call-start = ((), (), s32[]{:S(2)}) async-start(), calls=%async_computation.4 | async-start | bytes 6389760 | tf_op jit(solution)/shard_map/reduce_scatter | solution.py:102
  362.4 18.8 %copy-start.2 = (f32[1024,512]{1,0:T(8,128)S(1)}, f32[1024,512]{1,0:T(8,128)}, u32[]{:S(2)}) copy-start(f32[1024,512]{1,0:T(8,128)} %get-tuple-element.149) | copy-start | bytes 6291460
  362.4 18.8 %copy-start.4 = (f32[1024,512]{1,0:T(8,128)S(1)}, f32[1024,512]{1,0:T(8,128)}, u32[]{:S(2)}) copy-start(f32[1024,512]{1,0:T(8,128)} %get-tuple-element.116) | copy-start | bytes 6291460
  362.4 18.8 %copy-start.15 = (f32[512]{0:T(512)S(1)}, f32[512]{0:T(512)}, u32[]{:S(2)}) copy-start(f32[512]{0:T(512)} %copy-done.14) | copy-start | bytes 6148
  362.4 18.8 %copy-start.17 = (f32[512]{0:T(512)S(1)}, f32[512]{0:T(512)}, u32[]{:S(2)}) copy-start(f32[512]{0:T(512)} %copy-done.16) | copy-start | bytes 6148
  362.4 18.8 %copy-start.24 = (f32[1024]{0:T(1024)S(1)}, f32[1024]{0:T(1024)}, u32[]{:S(2)}) copy-start(f32[1024]{0:T(1024)} %copy-done.23) | copy-start | bytes 12292
  362.5 18.8 %copy-start.26 = (f32[1024]{0:T(1024)S(1)}, f32[1024]{0:T(1024)}, u32[]{:S(2)}) copy-start(f32[1024]{0:T(1024)} %copy-done.25) | copy-start | bytes 12292
  362.5 18.8 %copy-start.33 = (f32[512]{0:T(512)S(1)}, f32[512]{0:T(512)}, u32[]{:S(2)}) copy-start(f32[512]{0:T(512)} %copy-done.32) | copy-start | bytes 6148
  362.5 18.8 %copy-start.37 = (f32[1024]{0:T(1024)S(1)}, f32[1024]{0:T(1024)}, u32[]{:S(2)}) copy-start(f32[1024]{0:T(1024)} %copy-done.36) | copy-start | bytes 12292
  362.5 18.8 %copy-start.39 = (f32[1024]{0:T(1024)S(1)}, f32[1024]{0:T(1024)}, u32[]{:S(2)}) copy-start(f32[1024]{0:T(1024)} %copy-done.38) | copy-start | bytes 12292
  362.5 18.8 %copy-start.51 = (f32[1024]{0:T(1024)S(1)}, f32[1024]{0:T(1024)}, u32[]{:S(2)}) copy-start(f32[1024]{0:T(1024)} %copy-done.50) | copy-start | bytes 12292
  362.5 18.8 %copy-start.58 = (f32[1024,512]{1,0:T(8,128)S(1)}, f32[1024,512]{1,0:T(8,128)}, u32[]{:S(2)}) copy-start(f32[1024,512]{1,0:T(8,128)} %get-tuple-element.115) | copy-start | bytes 6291460
  381.3 53.8 %slice-start = ((s8[6291456]{0:T(1024)(128)(4,1)}), s8[4194304]{0:T(1024)(128)(4,1)S(1)}, s32[]{:S(2)}) async-start(s8[6291456]{0:T(1024)(128)(4,1)} %bitcast.102), calls=%async_computation.6 | async-start | bytes 8388608
  408.2 26.8 %slice-start.1 = ((s8[6291456]{0:T(1024)(128)(4,1)}), s8[2097152]{0:T(1024)(128)(4,1)S(1)}, s32[]{:S(2)}) async-start(s8[6291456]{0:T(1024)(128)(4,1)} %bitcast.102), calls=%async_computation.7 | async-start | bytes 4194304
  449.1 169.5 %copy-start.18 = (f32[8,512]{1,0:T(8,128)S(1)}, f32[8,512]{1,0:T(8,128)}, u32[]{:S(2)}) copy-start(f32[8,512]{1,0:T(8,128)} %get-tuple-element.109) | copy-start | bytes 49156
  607.0 10.2 %copy-start.9 = (f32[128,100]{0,1:T(8,128)S(1)}, f32[128,100]{0,1:T(8,128)}, u32[]{:S(2)}) copy-start(f32[128,100]{0,1:T(8,128)} %copy-done.8) | copy-start | bytes 153604
  607.0 10.2 %copy-start.12 = (f32[128,100]{0,1:T(8,128)S(1)}, f32[128,100]{0,1:T(8,128)}, u32[]{:S(2)}) copy-start(f32[128,100]{0,1:T(8,128)} %copy-done.11) | copy-start | bytes 153604
  632.4 253.6 %copy-start.43 = (f32[8]{0:T(128)S(1)}, f32[8]{0:T(128)}, u32[]{:S(2)}) copy-start(f32[8]{0:T(128)} %copy-done.42) | copy-start | bytes 100
  632.4 253.6 %copy-start.45 = (f32[8]{0:T(128)S(1)}, f32[8]{0:T(128)}, u32[]{:S(2)}) copy-start(f32[8]{0:T(128)} %copy-done.44) | copy-start | bytes 100
  632.4 253.6 %copy-start.47 = (f32[8]{0:T(128)S(1)}, f32[8]{0:T(128)}, u32[]{:S(2)}) copy-start(f32[8]{0:T(128)} %copy-done.46) | copy-start | bytes 100
  632.4 253.6 %copy-start.54 = (f32[8]{0:T(128)S(1)}, f32[8]{0:T(128)}, u32[]{:S(2)}) copy-start(f32[8]{0:T(128)} %copy-done.53) | copy-start | bytes 100
  632.4 295.8 %copy-start.7 = (bf16[8,3072]{1,0:T(8,128)(2,1)S(1)}, bf16[8,3072]{1,0:T(8,128)(2,1)}, u32[]{:S(2)}) copy-start(bf16[8,3072]{1,0:T(8,128)(2,1)} %param.8) | copy-start | bytes 147460
  632.4 295.8 %copy-start.28 = (f32[8]{0:T(128)S(1)}, f32[8]{0:T(128)}, u32[]{:S(2)}) copy-start(f32[8]{0:T(128)} %copy-done.27) | copy-start | bytes 100
  632.4 295.7 %copy-start.35 = (f32[8]{0:T(128)S(1)}, f32[8]{0:T(128)}, u32[]{:S(2)}) copy-start(f32[8]{0:T(128)} %copy-done.34) | copy-start | bytes 100
  632.4 295.7 %all-reduce.6.cloned.1.call-start = ((), (), s32[]{:S(2)}) async-start(), calls=%async_computation.5 | async-start | bytes 196608 | tf_op jit(solution)/shard_map/psum | solution.py:108
  (2 other events, 1.0 us)
Sparse Core Ops, SparseCore 0:
  11.3 86.4 all-gather.2
  103.3 72.3 all-gather.4
  362.5 244.4 all-reduce.3
  632.5 253.3 reduce-scatter.1
  888.5 39.5 all-reduce.5
where the time goes:
time: 942 us; the launch traced here: 937 us
  waiting for transfers between devices  493 us (52%)
  other arithmetic  201 us (21%)
  matrix products  116 us (12%)
  blocking collectives  78.1 us (8%)
  local copies, waits for them, and re-layouts  29.7 us (3%)
  between operations  19.5 us (2%)
    reduce_scatter x1, waiting for transfers between devices, body(): lax.psum_scatter(term_rows(jnp.int32(0), sup_rows * lax.axis_size('sup'))...  175 us
    psum x1, waiting for transfers between devices, body(): d_coeffs, loss_value = lax.psum((d_coeff_part, loss_part), ('tgt', 'sup'))  158 us
    another operation x15, other arithmetic, body(): factor = jnp.linalg.cholesky(system)  82 us
    all_gather x1, waiting for transfers between devices, body(): gathered = lax.all_gather(support_images, 'sup', axis=0, tiled=True)  82 us
    psum x1, blocking collectives, body(): d_coeffs, loss_value = lax.psum((d_coeff_part, loss_part), ('tgt', 'sup'))  78.1 us
    reduce_sum x7, other arithmetic, ntk_kernel(): spread = (1.0 + 2.0 * norm_row) * (1.0 + 2.0 * norm_col)  44.1 us
    another operation x4, other arithmetic, ridge_solve(): lax.linalg.triangular_solve(factor, middle, left_side=True, lower=True, t...  43.1 us
    psum x1, waiting for transfers between devices, body(): summed = lax.psum(partial_rows, 'tgt')  42.1 us
  transfers between devices with their start and end apart: 5, of which 5 were waited for; matrix products, arithmetic and copies ran while one was open for 14% of the time, Pallas kernels for 0%

commit v1 on v0

--- a/solution.py
+++ b/solution.py
@@ -105,7 +105,7 @@
         scatter_dimension=0,
         tiled=True,
     )
-    summed = lax.psum(partial_rows, "tgt")
+    summed = jnp.sum(lax.all_gather(partial_rows, "tgt"), axis=0)
     local_rows = jnp.dot(coef_ss, gathered, preferred_element_type=jnp.float32)
     local_rows = local_rows + 2.0 / D * qrow_ss * support_images.astype(jnp.float32)
     return (total_sup * (summed + local_rows), loss_value)

time: 942 us -> 908 us (0.964)
  waiting for transfers between devices: 493 us -> 450 us
    psum x1 -> x0, waiting for transfers between devices: 42.1 us -> none  [body(): summed = lax.psum(partial_rows, 'tgt')]
  transfers between devices with their start and end apart: 5 -> 4, of which waited for: 5 -> 4; matrix products, arithmetic and copies ran while one was open for 14% -> 14% of each run, Pallas kernels for 0% -> 0%
where the time goes in v1:
time: 908 us; the launch traced here: 903 us
  waiting for transfers between devices  450 us (50%)
  other arithmetic  201 us (22%)
  matrix products  115 us (13%)
  blocking collectives  86.9 us (10%)
  local copies, waits for them, and re-layouts  30.2 us (3%)
  between operations  19.4 us (2%)
    reduce_scatter x1, waiting for transfers between devices, body(): lax.psum_scatter(term_rows(jnp.int32(0), sup_rows * lax.axis_size('sup'))...  175 us
    psum x1, waiting for transfers between devices, body(): d_coeffs, loss_value = lax.psum((d_coeff_part, loss_part), ('tgt', 'sup'))  158 us
    another operation x15, other arithmetic, body(): factor = jnp.linalg.cholesky(system)  82.1 us
    all_gather x1, waiting for transfers between devices, body(): gathered = lax.all_gather(support_images, 'sup', axis=0, tiled=True)  81.9 us
    psum x1, blocking collectives, body(): d_coeffs, loss_value = lax.psum((d_coeff_part, loss_part), ('tgt', 'sup'))  78.2 us
    reduce_sum x7, other arithmetic, ntk_kernel(): spread = (1.0 + 2.0 * norm_row) * (1.0 + 2.0 * norm_col)  44.2 us
    another operation x4, other arithmetic, ridge_solve(): lax.linalg.triangular_solve(factor, middle, left_side=True, lower=True, t...  43.1 us
    dot_general x1, matrix products, body(): lax.dot_general(target_images, gathered, contract, preferred_element_type...  37 us
  transfers between devices with their start and end apart: 4, of which 4 were waited for; matrix products, arithmetic and copies ran while one was open for 14% of the time, Pallas kernels for 0%

profile of v1, /device:TPU:1, one launch (start us, length us, event | category | flops | bytes accessed | tf_op | source)
XLA Modules:
  0.0 903.1 jit_solution(9569594725158152154)
XLA Ops:
  10.7 4.1 multiply_reduce_fusion
  15.9 81.9 %all-gather.4.cloned.1.call-done = bf16[512,3072]{1,0:T(8,128)(2,1)} async-done(((bf16[8,3072]{1,0:T(8,128)(2,1)}), bf16[512,3072]{1,0:T(8,128)(2,1)}) %all-gather.4.cloned.1.call-update) | async-done | bytes 3145744 | tf_op jit(solution)/shard_map/all_gather | solution.py:57
  97.8 2.7 fusion
  101.3 1.8 multiply_add_fusion.5
  103.5 37.0 %multiply_add_fusion = (f32[1024,512]{1,0:T(8,128)}, f32[1024,512]{1,0:T(8,128)}, f32[1024,512]{1,0:T(8,128)}, f32[1024,512]{1,0:T(8,128)}) fusion(f32[512]{0:T(512)S(1)} %get-tuple-element.154, f32[1024]{0:T(1024)S(1)} %multiply_add_fusion.10, f32[512]{0:T(512)S(1)} %get-tuple-element.119, f32[1024]{0:T(1024)S(1)} %get-tuple-element.135, ...), kind=kOutput, calls=%fused_computation.109 | convolution fusion | flops 3261071360 | bytes 17856512 | tf_op jit(solution)/shard_map/dot_general | solution.py:62
  140.5 35.2 %all-gather.6.cloned.1.call-done = f32[512,512]{1,0:T(8,128)} async-done(((f32[8,512]{1,0:T(8,128)}), f32[512,512]{1,0:T(8,128)}) %all-gather.6.cloned.1.call-update) | async-done | bytes 1048592 | tf_op jit(solution)/shard_map/all_gather | solution.py:69
  175.7 2.5 copy.23
  178.2 1.9 select_reduce_fusion
  180.8 2.3 select_add_fusion
  183.1 2.6 copy.24
  185.7 1.8 fusion.99
  187.5 1.1 copy-done.3
  188.6 11.7 %cholesky.103 = f32[128,128]{1,0:T(8,128)S(1)} custom-call(f32[128,128]{1,0:T(8,128)S(1)} %cholesky.263), custom_call_target="Cholesky" | custom-call | tf_op jit(solution)/shard_map/jit(cholesky)/cholesky | solution.py:72
  200.9 9.8 %custom-call.33 = f32[1,128,128]{1,2,0:T(8,128)S(1)} custom-call(f32[1,128,128]{2,1,0:T(8,128)S(1)} %get-tuple-element.131), custom_call_target="InvertDiagBlocksLowerTriangular" | custom-call | tf_op jit(solution)/shard_map/jit(cholesky)/cholesky | solution.py:72
  210.7 1.2 fusion.110
  212.0 1.3 convolution_subtract_fusion.1
  213.9 11.7 %cholesky.215 = f32[128,128]{1,0:T(8,128)S(1)} custom-call(f32[128,128]{1,0:T(8,128)S(1)} %cholesky.267), custom_call_target="Cholesky" | custom-call | tf_op jit(solution)/shard_map/jit(cholesky)/cholesky | solution.py:72
  225.7 1.2 select_reduce_fusion.3
  228.7 1.1 cholesky.222
  229.8 11.0 %custom-call.34 = f32[1,128,128]{1,2,0:T(8,128)S(1)} custom-call(f32[1,128,128]{2,1,0:T(8,128)} %get-tuple-element.129), custom_call_target="InvertDiagBlocksLowerTriangular" | custom-call | tf_op jit(solution)/shard_map/jit(cholesky)/cholesky | solution.py:72
  241.5 1.5 constant_dynamic-update-slice_fusion.2
  243.0 1.9 convolution_dynamic-update-slice_fusion
  244.9 1.6 convolution_subtract_fusion.2
  246.5 11.7 %cholesky.236 = f32[128,128]{1,0:T(8,128)S(1)} custom-call(f32[128,128]{1,0:T(8,128)S(1)} %cholesky.272), custom_call_target="Cholesky" | custom-call | tf_op jit(solution)/shard_map/jit(cholesky)/cholesky | solution.py:72
  259.0 9.8 %custom-call.35 = f32[1,128,128]{1,2,0:T(8,128)S(1)} custom-call(f32[1,128,128]{2,1,0:T(8,128)S(1)} %get-tuple-element.127), custom_call_target="InvertDiagBlocksLowerTriangular" | custom-call | tf_op jit(solution)/shard_map/jit(cholesky)/cholesky | solution.py:72
  269.7 1.5 convolution_subtract_fusion.6
  271.3 11.9 %cholesky.253 = f32[128,128]{1,0:T(8,128)S(1)} custom-call(f32[128,128]{1,0:T(8,128)S(1)} %convolution_subtract_fusion.6), custom_call_target="Cholesky" | custom-call | tf_op jit(solution)/shard_map/jit(cholesky)/cholesky | solution.py:72
  289.0 2.4 select_select_fusion
  291.4 14.8 %while.8 = (s32[]{:T(128)}, f32[512,512]{0,1:T(8,128)}, s32[4,2]{0,1:T(2,128)S(1)}, f32[4,128,128]{2,1,0:T(8,128)}, s32[]{:T(128)}) while((s32[]{:T(128)}, f32[512,512]{0,1:T(8,128)}, s32[4,2]{0,1:T(2,128)S(1)}, f32[4,128,128]{2,1,0:T(8,128)}, s32[]{:T(128)}) %tuple.98), condition=%wide.while_cond.1, body=%wide.while_body.1.sunk | while | flops 2 | bytes 393829 | solution.py:29
  292.1 2.3 dynamic-slice.14
  295.8 2.3 dynamic-slice.14
  299.6 2.3 dynamic-slice.14
  303.3 2.3 dynamic-slice.14
  306.3 40.1 %custom-call.39 = f32[4,128,128]{1,2,0:T(8,128)S(1)} custom-call(f32[4,128,128]{2,1,0:T(8,128)} %get-tuple-element.33), custom_call_target="InvertDiagBlocksLowerTriangular" | custom-call | tf_op jit(solution)/shard_map/triangular_solve/custom-call.8 | solution.py:29
  346.4 1.3 fusion.155
  347.7 1.2 convolution_subtract_fusion.4
  349.2 1.3 convolution_subtract_fusion.3
  350.8 1.4 convolution_subtract_fusion.5
  352.8 1.1 convolution_subtract_fusion.12
  354.1 1.2 convolution_subtract_fusion.11
  355.6 1.3 convolution_subtract_fusion.15
  357.2 2.8 multiply_reduce_fusion.1
  360.8 2.1 fusion.102
  363.1 18.7 %fusion.81 = (f32[1024,512]{1,0:T(8,128)S(1)}, f32[1024,512]{1,0:T(8,128)S(1)}, f32[1024,512]{1,0:T(8,128)S(1)}) fusion(f32[512]{0:T(512)} %copy-done.32, f32[1024]{0:T(1024)} %copy-done.50, f32[512]{0:T(512)S(1)} %copy-done.20, f32[1024]{0:T(1024)} %copy-done.38, f32[1024,512]{1,0:T(8,128)} %get-tuple-element.115, f32[512]{0:T(512)S(1)} %copy-done.22, ...), kind=kOutput, calls=%fused_computation.97 | convolution fusion | flops 658761728 | bytes 11118592 | tf_op jit(solution)/shard_map/dot_general | solution.py:92
  381.9 26.9 %fusion.92 = (f32[512]{0:T(512)}, f32[512]{0:T(512)}, f32[512]{0:T(512)}, f32[1024,512]{1,0:T(8,128)S(1)}, f32[1024,512]{1,0:T(8,128)S(1)}) fusion(f32[512]{0:T(512)S(1)} %copy-done.33, f32[1024]{0:T(1024)S(1)} %copy-done.51, f32[1024,512]{1,0:T(8,128)S(1)} %get-tuple-element.151, f32[1024,512]{1,0:T(8,128)S(1)} %copy-done.58, f32[512]{0:T(512)S(1)} %copy-done.20, ...), kind=kLoop, calls=%fused_computation.128 | loop fusion | flops 67107328 | bytes 16814080 | tf_op jit(solution)/shard_map/transpose(jvp())/reduce_sum | solution.py:17
  408.8 14.4 %fusion.61 = (f32[1024,512]{1,0:T(8,128)S(1)}, f32[1024,512]{1,0:T(8,128)S(1)}) fusion(f32[1024,512]{1,0:T(8,128)S(1)} %get-tuple-element.92, f32[1024,512]{1,0:T(8,128)S(1)} %get-tuple-element.91, f32[1024,512]{1,0:T(8,128)S(1)} %copy-done.4, f32[512]{0:T(512)S(1)} %copy-done.22, f32[1024]{0:T(1024)S(1)} %copy-done.37, f32[512]{0:T(512)S(1)} %copy-done.17, ...), kind=kLoop, calls=%fused_computation.77 | loop fusion | flops 24117248 | bytes 14704640 | tf_op jit(solution)/shard_map/transpose(jvp())/mul | solution.py:18
  423.2 12.5 %fusion.89 = (f32[512]{0:T(512)}, f32[512]{0:T(512)}, f32[1024,512]{1,0:T(8,128)S(1)}) fusion(f32[1024,512]{1,0:T(8,128)S(1)} %get-tuple-element.103, f32[512]{0:T(512)S(1)} %copy-done.17, f32[1024]{0:T(1024)S(1)} %copy-done.26, f32[1024,512]{1,0:T(8,128)S(1)} %get-tuple-element.104, f32[1024,512]{1,0:T(8,128)S(1)} %copy-done.2, f32[512]{0:T(512)S(1)} %copy-done.15, ...), kind=kLoop, calls=%fused_computation.125 | loop fusion | flops 36699136 | bytes 8404992 | tf_op jit(solution)/shard_map/transpose(jvp())/reduce_sum | solution.py:17
  435.6 14.1 %fusion.100 = f32[512,3072]{1,0:T(8,128)} fusion(bf16[1024,3072]{1,0:T(8,128)(2,1)S(1)} %bitcast.105, f32[1024,512]{1,0:T(8,128)S(1)} %get-tuple-element.93, f32[1024,512]{1,0:T(8,128)S(1)} %copy-done.2, f32[512]{0:T(512)S(1)} %copy-done.15, f32[1024]{0:T(1024)S(1)} %copy-done.24, f32[1024,512]{1,0:T(8,128)S(1)} %get-tuple-element.104, ...), kind=kOutput, calls=%fused_computation.161 | convolution fusion | flops 3242196992 | bytes 18886656 | tf_op jit(solution)/shard_map/dot_general | solution.py:38
  449.7 157.8 %all-reduce.3.cloned.1.call-done = f32[512,100]{0,1:T(8,128)} async-done(((f32[512,100]{0,1:T(8,128)}), f32[512,100]{0,1:T(8,128)}) %all-reduce.3.cloned.1.call-update) | async-done | bytes 204816 | tf_op jit(solution)/shard_map/psum | solution.py:81
  607.5 1.1 fusion.166
  608.6 1.1 convolution_subtract_fusion.10
  609.9 1.2 convolution_subtract_fusion.9
  611.5 1.3 convolution_subtract_fusion.14
  613.3 1.1 convolution_subtract_fusion.8
  614.7 1.2 convolution_subtract_fusion.7
  616.1 1.3 convolution_subtract_fusion.13
  619.0 1.3 fusion.209
  620.2 1.1 multiply_reduce_fusion.6
  621.3 1.1 multiply_reduce_fusion.5
  625.9 6.9 fusion.1
  633.6 78.2 %psum.15 = f32[]{:T(128)} all-reduce(f32[]{:T(128)S(6)} %div.757), channel_id=1, replica_groups=mesh['tgt'=4,'sup'=64] {'tgt','sup'}, use_global_device_ids=true, to_apply=%region_32.35 | all-reduce | flops 1 | bytes 8 | tf_op jit(solution)/shard_map/psum | solution.py:81
  711.8 174.5 %reduce-scatter.2.cloned.1.call-done = f32[8,3072]{1,0:T(8,128)} async-done(((f32[512,3072]{1,0:T(8,128)}), f32[8,3072]{1,0:T(8,128)}) %reduce-scatter.2.cloned.1.call-update) | async-done | bytes 98320 | tf_op jit(solution)/shard_map/reduce_scatter | solution.py:102
  886.3 8.7 all-gather
  895.1 1.3 fusion.3
  (199 shorter events, 28.9 us)
Async XLA Ops:
  7.2 90.6 %all-gather.4.cloned.1.call-start = ((), (), s32[]{:S(2)}) async-start(), calls=%async_computation.1 | async-start | bytes 3194880 | tf_op jit(solution)/shard_map/all_gather | solution.py:57
  7.9 167.8 %all-gather.6.cloned.1.call-start = ((), (), s32[]{:S(2)}) async-start(), calls=%async_computation.2 | async-start | bytes 1064960 | tf_op jit(solution)/shard_map/all_gather | solution.py:69
  10.1 0.6 copy-start.44
  10.1 0.6 copy-start.46
  10.1 4.7 copy-start.53
  10.1 91.2 %copy-start.27 = (f32[8]{0:T(128)}, f32[8]{0:T(128)S(1)}, u32[]{:S(2)}) copy-start(f32[8]{0:T(128)S(1)} %get-tuple-element.148) | copy-start | bytes 100
  10.2 91.2 %copy-start.40 = (f32[8]{0:T(128)}, f32[8]{0:T(128)S(1)}, u32[]{:S(2)}) copy-start(f32[8]{0:T(128)S(1)} %get-tuple-element.110) | copy-start | bytes 100
  10.2 91.1 %copy-start.34 = (f32[8]{0:T(128)}, f32[8]{0:T(128)S(1)}, u32[]{:S(2)}) copy-start(f32[8]{0:T(128)S(1)} %broadcast_add_fusion.8) | copy-start | bytes 100
  10.7 90.6 %copy-start.41 = (f32[8]{0:T(128)}, f32[8]{0:T(128)S(1)}, u32[]{:S(2)}) copy-start(f32[8]{0:T(128)S(1)} %get-tuple-element.156) | copy-start | bytes 100
  10.7 90.6 %copy-start.48 = (f32[8]{0:T(128)}, f32[8]{0:T(128)S(1)}, u32[]{:S(2)}) copy-start(f32[8]{0:T(128)S(1)} %get-tuple-element.155) | copy-start | bytes 100
  10.7 4.4 copy-start.52
  14.8 86.5 %copy-start.6 = (bf16[8,3072]{1,0:T(8,128)(2,1)S(1)}, bf16[8,3072]{1,0:T(8,128)(2,1)}, u32[]{:S(2)}) copy-start(bf16[8,3072]{1,0:T(8,128)(2,1)} %param.8) | copy-start | bytes 147460
  15.0 88.4 %copy-start.23 = (f32[1024]{0:T(1024)}, f32[1024]{0:T(1024)S(1)}, u32[]{:S(2)}) copy-start(f32[1024]{0:T(1024)S(1)} %get-tuple-element.133) | copy-start | bytes 12292
  15.0 88.4 %copy-start.25 = (f32[1024]{0:T(1024)}, f32[1024]{0:T(1024)S(1)}, u32[]{:S(2)}) copy-start(f32[1024]{0:T(1024)S(1)} %get-tuple-element.137) | copy-start | bytes 12292
  15.0 88.4 %copy-start.36 = (f32[1024]{0:T(1024)}, f32[1024]{0:T(1024)S(1)}, u32[]{:S(2)}) copy-start(f32[1024]{0:T(1024)S(1)} %get-tuple-element.134) | copy-start | bytes 12292
  15.0 88.4 %copy-start.38 = (f32[1024]{0:T(1024)}, f32[1024]{0:T(1024)S(1)}, u32[]{:S(2)}) copy-start(f32[1024]{0:T(1024)S(1)} %get-tuple-element.135) | copy-start | bytes 12292
  15.1 88.4 %copy-start.50 = (f32[1024]{0:T(1024)}, f32[1024]{0:T(1024)S(1)}, u32[]{:S(2)}) copy-start(f32[1024]{0:T(1024)S(1)} %multiply_add_fusion.10) | copy-start | bytes 12292
  97.8 3.5 copy-start
  100.5 0.6 copy-start.31
  100.7 0.5 copy-start.29
  100.7 0.6 copy-start.30
  100.7 39.7 %copy-start.14 = (f32[512]{0:T(512)}, f32[512]{0:T(512)S(1)}, u32[]{:S(2)}) copy-start(f32[512]{0:T(512)S(1)} %get-tuple-element.145) | copy-start | bytes 6148
  100.7 39.7 %copy-start.19 = (f32[512]{0:T(512)}, f32[512]{0:T(512)S(1)}, u32[]{:S(2)}) copy-start(f32[512]{0:T(512)S(1)} %get-tuple-element.119) | copy-start | bytes 6148
  101.2 39.3 %copy-start.16 = (f32[512]{0:T(512)}, f32[512]{0:T(512)S(1)}, u32[]{:S(2)}) copy-start(f32[512]{0:T(512)S(1)} %get-tuple-element.146) | copy-start | bytes 6148
  101.2 39.3 %copy-start.21 = (f32[512]{0:T(512)}, f32[512]{0:T(512)S(1)}, u32[]{:S(2)}) copy-start(f32[512]{0:T(512)S(1)} %get-tuple-element.147) | copy-start | bytes 6148
  101.2 39.3 %copy-start.32 = (f32[512]{0:T(512)}, f32[512]{0:T(512)S(1)}, u32[]{:S(2)}) copy-start(f32[512]{0:T(512)S(1)} %get-tuple-element.154) | copy-start | bytes 6148
  103.2 504.3 %all-reduce.3.cloned.1.call-start = ((), (), s32[]{:S(2)}) async-start(), calls=%async_computation.3 | async-start | bytes 425984 | tf_op jit(solution)/shard_map/psum | solution.py:81
  187.5 1.1 copy-start.3
  200.3 0.6 copy-start.13
  213.2 0.7 copy-start.10
  241.5 41.8 %copy-start.56 = (f32[128]{0:T(128)S(1)}, f32[128]{0:T(128)}, u32[]{:S(2)}) copy-start(f32[128]{0:T(128)} %get-tuple-element.128) | copy-start | bytes 1540
  241.5 42.4 %copy-start.55 = (f32[128]{0:T(128)S(1)}, f32[128]{0:T(128)}, u32[]{:S(2)}) copy-start(f32[128]{0:T(128)} %get-tuple-element.130) | copy-start | bytes 1540
  244.8 46.6 %copy-start.57 = (s32[4]{0:T(128)S(1)}, s32[4]{0:T(128)}, u32[]{:S(2)}) copy-start(s32[4]{0:T(128)} %iota_multiply_fusion) | copy-start | bytes 52
  306.3 50.9 %copy-start.49 = (s32[1024]{0:T(1024)S(1)}, s32[1024]{0:T(1024)}, u32[]{:S(2)}) copy-start(s32[1024]{0:T(1024)} %param.11) | copy-start | bytes 12292
  346.4 10.8 %copy-start.1 = (f32[1024,512]{1,0:T(8,128)S(1)}, f32[1024,512]{1,0:T(8,128)}, u32[]{:S(2)}) copy-start(f32[1024,512]{1,0:T(8,128)} %get-tuple-element.114) | copy-start | bytes 6291460
  355.6 1.6 copy-start.8
  357.1 2.9 copy-start.11
  360.0 0.8 copy-start.5
  360.0 2.9 copy-start.20
  360.0 2.9 copy-start.22
  362.9 523.4 %reduce-scatter.2.cloned.1.call-start = ((), (), s32[]{:S(2)}) async-start(), calls=%async_computation.4 | async-start | bytes 6389760 | tf_op jit(solution)/shard_map/reduce_scatter | solution.py:102
  362.9 18.8 %copy-start.2 = (f32[1024,512]{1,0:T(8,128)S(1)}, f32[1024,512]{1,0:T(8,128)}, u32[]{:S(2)}) copy-start(f32[1024,512]{1,0:T(8,128)} %get-tuple-element.149) | copy-start | bytes 6291460
  363.0 18.8 %copy-start.4 = (f32[1024,512]{1,0:T(8,128)S(1)}, f32[1024,512]{1,0:T(8,128)}, u32[]{:S(2)}) copy-start(f32[1024,512]{1,0:T(8,128)} %get-tuple-element.116) | copy-start | bytes 6291460
  363.0 18.8 %copy-start.15 = (f32[512]{0:T(512)S(1)}, f32[512]{0:T(512)}, u32[]{:S(2)}) copy-start(f32[512]{0:T(512)} %copy-done.14) | copy-start | bytes 6148
  363.0 18.8 %copy-start.17 = (f32[512]{0:T(512)S(1)}, f32[512]{0:T(512)}, u32[]{:S(2)}) copy-start(f32[512]{0:T(512)} %copy-done.16) | copy-start | bytes 6148
  363.0 18.8 %copy-start.24 = (f32[1024]{0:T(1024)S(1)}, f32[1024]{0:T(1024)}, u32[]{:S(2)}) copy-start(f32[1024]{0:T(1024)} %copy-done.23) | copy-start | bytes 12292
  363.0 18.8 %copy-start.26 = (f32[1024]{0:T(1024)S(1)}, f32[1024]{0:T(1024)}, u32[]{:S(2)}) copy-start(f32[1024]{0:T(1024)} %copy-done.25) | copy-start | bytes 12292
  363.0 18.8 %copy-start.33 = (f32[512]{0:T(512)S(1)}, f32[512]{0:T(512)}, u32[]{:S(2)}) copy-start(f32[512]{0:T(512)} %copy-done.32) | copy-start | bytes 6148
  363.0 18.8 %copy-start.37 = (f32[1024]{0:T(1024)S(1)}, f32[1024]{0:T(1024)}, u32[]{:S(2)}) copy-start(f32[1024]{0:T(1024)} %copy-done.36) | copy-start | bytes 12292
  363.0 18.8 %copy-start.39 = (f32[1024]{0:T(1024)S(1)}, f32[1024]{0:T(1024)}, u32[]{:S(2)}) copy-start(f32[1024]{0:T(1024)} %copy-done.38) | copy-start | bytes 12292
  363.0 18.8 %copy-start.51 = (f32[1024]{0:T(1024)S(1)}, f32[1024]{0:T(1024)}, u32[]{:S(2)}) copy-start(f32[1024]{0:T(1024)} %copy-done.50) | copy-start | bytes 12292
  363.0 18.8 %copy-start.58 = (f32[1024,512]{1,0:T(8,128)S(1)}, f32[1024,512]{1,0:T(8,128)}, u32[]{:S(2)}) copy-start(f32[1024,512]{1,0:T(8,128)} %get-tuple-element.115) | copy-start | bytes 6291460
  381.9 53.8 %slice-start = ((s8[6291456]{0:T(1024)(128)(4,1)}), s8[4194304]{0:T(1024)(128)(4,1)S(1)}, s32[]{:S(2)}) async-start(s8[6291456]{0:T(1024)(128)(4,1)} %bitcast.104), calls=%async_computation.5 | async-start | bytes 8388608
  408.8 26.9 %slice-start.1 = ((s8[6291456]{0:T(1024)(128)(4,1)}), s8[2097152]{0:T(1024)(128)(4,1)S(1)}, s32[]{:S(2)}) async-start(s8[6291456]{0:T(1024)(128)(4,1)} %bitcast.104), calls=%async_computation.6 | async-start | bytes 4194304
  449.7 169.3 %copy-start.18 = (f32[8,512]{1,0:T(8,128)S(1)}, f32[8,512]{1,0:T(8,128)}, u32[]{:S(2)}) copy-start(f32[8,512]{1,0:T(8,128)} %get-tuple-element.109) | copy-start | bytes 49156
  607.5 10.2 %copy-start.9 = (f32[128,100]{0,1:T(8,128)S(1)}, f32[128,100]{0,1:T(8,128)}, u32[]{:S(2)}) copy-start(f32[128,100]{0,1:T(8,128)} %copy-done.8) | copy-start | bytes 153604
  607.5 10.2 %copy-start.12 = (f32[128,100]{0,1:T(8,128)S(1)}, f32[128,100]{0,1:T(8,128)}, u32[]{:S(2)}) copy-start(f32[128,100]{0,1:T(8,128)} %copy-done.11) | copy-start | bytes 153604
  632.8 78.9 %copy-start.43 = (f32[8]{0:T(128)S(1)}, f32[8]{0:T(128)}, u32[]{:S(2)}) copy-start(f32[8]{0:T(128)} %copy-done.42) | copy-start | bytes 100
  632.8 78.9 %copy-start.45 = (f32[8]{0:T(128)S(1)}, f32[8]{0:T(128)}, u32[]{:S(2)}) copy-start(f32[8]{0:T(128)} %copy-done.44) | copy-start | bytes 100
  632.8 78.9 %copy-start.47 = (f32[8]{0:T(128)S(1)}, f32[8]{0:T(128)}, u32[]{:S(2)}) copy-start(f32[8]{0:T(128)} %copy-done.46) | copy-start | bytes 100
  632.8 78.9 %copy-start.54 = (f32[8]{0:T(128)S(1)}, f32[8]{0:T(128)}, u32[]{:S(2)}) copy-start(f32[8]{0:T(128)} %copy-done.53) | copy-start | bytes 100
  632.8 262.2 %copy-start.7 = (bf16[8,3072]{1,0:T(8,128)(2,1)S(1)}, bf16[8,3072]{1,0:T(8,128)(2,1)}, u32[]{:S(2)}) copy-start(bf16[8,3072]{1,0:T(8,128)(2,1)} %param.8) | copy-start | bytes 147460
  632.9 262.2 %copy-start.28 = (f32[8]{0:T(128)S(1)}, f32[8]{0:T(128)}, u32[]{:S(2)}) copy-start(f32[8]{0:T(128)} %copy-done.27) | copy-start | bytes 100
  632.9 262.2 %copy-start.35 = (f32[8]{0:T(128)S(1)}, f32[8]{0:T(128)}, u32[]{:S(2)}) copy-start(f32[8]{0:T(128)} %copy-done.34) | copy-start | bytes 100
  (1 other events, 0.5 us)
Sparse Core Ops, SparseCore 0:
  11.3 86.4 all-gather.3
  103.3 72.3 all-gather.5
  363.0 244.4 all-reduce.2
  633.0 253.2 reduce-scatter.1
